TPU v7x, 512 devices: a whole 4x8x8 slice. The times are simulated.
512 devices in a mesh: img: 8 (over y_lo, core), cin: 8 (over x, y_hi), cout: 8 (over z).
Axes of the slice: x: 4, y: 8 (y_hi: 2, y_lo: 4; y = y_hi * 4 + y_lo), z: 8, core: 2. Of those that a mesh axis runs over, the one named last changes fastest.
Arguments:
- maps: bfloat16 [2, 8, 14, 14, 1024], P(None, 'img'), may hold values from -6 to 6
- w_first: bfloat16 [3, 3, 1024, 1024], P(None, None, 'cin', 'cout'), may hold values from -0.09375 to 0.09375
- w_reduce: bfloat16 [3, 3, 1024, 8192], P(None, None, 'img', ('cin', 'cout')), may hold values from -0.09375 to 0.09375
- w_wide: bfloat16 [3, 3, 8192, 8192], P(None, None, 'cin', ('img', 'cout')), may hold values from -0.03125 to 0.03125
Outputs:
- wide_out: bfloat16 [2, 8, 7, 7, 8192], P(None, 'cin', None, None, ('img', 'cout'))
All inputs are finite; a program needn't handle non-finite values.
Results may differ from a plain program's by a relative error of at most 0.014.
Values may be sent and summed in bfloat16 or wider, within the bound.
No kernel may reach another device: no remote copies, remote signals or barrier semaphores. Data moves between devices by JAX's collectives and lax.ppermute only.
A program may use at most 64 MiB of HBM per device.

v0:
```python
import jax
import jax.numpy as jnp
from jax import lax
from jax.sharding import PartitionSpec as P


def conv_block(padded, weight_flat, size, step):
    channels = padded.shape[3]
    windows = []
    for row_tap in range(3):
        for col_tap in range(3):
            windows.append(
                padded[
                    :,
                    row_tap : row_tap + step * (size - 1) + 1 : step,
                    col_tap : col_tap + step * (size - 1) + 1 : step,
                    :,
                ]
            )
    table = jnp.concatenate(windows, axis=3).reshape(-1, 9 * channels)
    total = jnp.dot(table, weight_flat, preferred_element_type=jnp.float32)
    return total.reshape(padded.shape[0], size, size, weight_flat.shape[1])


def conv_taps(padded, weight, size, step):
    count = padded.shape[0]
    channels = padded.shape[3]
    weight_flat = weight.reshape(9 * channels, weight.shape[3])
    group = 1
    for trial in range(1, 9):
        if count % trial == 0:
            group = trial
    blocks = padded.reshape(count // group, group, padded.shape[1], padded.shape[2], channels)
    results = lax.map(lambda block: conv_block(block, weight_flat, size, step), blocks)
    return results.reshape(count, size, size, weight.shape[3])


def pad_map(values):
    return jnp.pad(values, ((0, 0), (1, 1), (1, 1), (0, 0)))


def local(maps, w_first, w_reduce, w_wide):
    batches = maps.shape[0]
    side = maps.shape[2]
    half = side // 2
    in_block = w_first.shape[2]
    out_block = w_first.shape[3]
    flat = maps.reshape(-1, side, side, maps.shape[4])
    in_part = lax.dynamic_slice_in_dim(flat, lax.axis_index("cin") * in_block, in_block, 3)
    first_terms = conv_taps(pad_map(jnp.maximum(in_part, 0)), w_first, side, 1)
    first_terms = first_terms.reshape(batches, maps.shape[1], side, side, out_block)
    summed = lax.psum(first_terms, "cin")
    own_part = lax.dynamic_slice_in_dim(maps, lax.axis_index("cout") * out_block, out_block, 4)
    segment_maps = (own_part.astype(jnp.float32) + summed).astype(jnp.bfloat16)
    whole = lax.all_gather(segment_maps, "cout", axis=4, tiled=True)
    by_channel = lax.all_to_all(whole, "img", split_axis=4, concat_axis=1, tiled=True)
    images = by_channel.shape[1]
    rect_segment = jnp.maximum(by_channel, 0).reshape(-1, side, side, by_channel.shape[4])
    reduced = conv_taps(pad_map(rect_segment), w_reduce, half, 2).reshape(
        batches, images, half, half, w_reduce.shape[3]
    )
    out_width = w_wide.shape[3]
    summed_wide = lax.psum(reduced, "img")
    narrow = jnp.maximum(summed_wide, 0.0).astype(jnp.bfloat16)
    gathered = lax.all_gather(narrow, "cout", axis=4, tiled=True)
    flat_all = gathered.reshape(-1, half, half, gathered.shape[4])
    partial_value = conv_taps(pad_map(flat_all), w_wide, half, 1)
    partial_value = partial_value.reshape(batches, images, half, half, out_width)
    result = lax.psum_scatter(
        partial_value.astype(jnp.bfloat16), "cin", scatter_dimension=1, tiled=True
    )
    return result


def solution(mesh):
    in_specs = (
        P(None, "img", None, None, None),
        P(None, None, "cin", "cout"),
        P(None, None, "img", ("cin", "cout")),
        P(None, None, "cin", ("img", "cout")),
    )
    out_specs = P(None, "cin", None, None, ("img", "cout"))
    return jax.shard_map(local, mesh=mesh, in_specs=in_specs, out_specs=out_specs, check_vma=False)
```

profile of v0, /device:TPU:64, one launch (start us, length us, event | category | flops | bytes accessed | tf_op | source)
XLA Modules:
  0.0 461.7 jit_solution(14591765025077755233)
XLA Ops:
  9.3 116.6 %all-reduce.8.cloned.1.call-done = f32[2,1,14,14,128]{4,3,2,0,1:T(8,128)} async-done(((f32[2,1,14,14,128]{4,3,2,0,1:T(8,128)}), f32[2,1,14,14,128]{4,3,2,0,1:T(8,128)}) %all-reduce.8.cloned.1.call-update) | async-done | bytes 200720 | tf_op jit(solution)/shard_map/psum | solution.py:52
  126.9 26.5 %all_gather.6 = bf16[2,1,14,14,1024]{4,3,2,0,1:T(8,128)(2,1)S(1)} all-gather(bf16[2,1,14,14,128]{4,3,2,0,1:T(8,128)(2,1)S(1)} %add_convert_fusion), channel_id=1, replica_groups=mesh['img'=8,'cin'=8,'cout'=8] {'cout'}, dimensions={4}, use_global_device_ids=true | all-gather | bytes 903168 | tf_op jit(solution)/shard_map/all_gather | solution.py:55
  153.5 12.4 %copy.42 = bf16[2,1,14,14,1024]{3,0,2,1,4:T(2,128)(2,1)} copy(bf16[2,1,14,14,1024]{4,3,2,0,1:T(8,128)(2,1)S(1)} %all_gather.6) | data formatting | bytes 1605632 | tf_op jit(solution)/shard_map/all_gather | solution.py:55
  165.8 12.8 %reshape.68 = bf16[8,2,25088]{2,1,0:T(2,128)(2,1)} reshape(bf16[1024,1,14,2,14]{4,3,2,1,0:T(2,128)(2,1)} %bitcast.84) | data formatting | bytes 1605632
  178.7 3.5 all-to-all-start
  182.3 21.2 %all-to-all-done = bf16[8,2,25088]{2,1,0:T(2,128)(2,1)S(1)} async-done(((bf16[8,2,25088]{2,1,0:T(2,128)(2,1)}), bf16[8,2,25088]{2,1,0:T(2,128)(2,1)S(1)}, u32[]{:S(2)}, u32[]{:S(2)}) %all-to-all-start) | async-done | bytes 802848 | tf_op jit(solution)/shard_map/all_to_all | solution.py:56
  203.4 19.8 %reshape.69 = bf16[1024,1,14,2,14]{4,3,2,1,0:T(2,128)(2,1)} reshape(bf16[8,2,25088]{2,1,0:T(2,128)(2,1)S(1)} %all-to-all-done) | data formatting | bytes 1605632
  223.2 17.3 %copy.43 = bf16[2,1,14,14,1024]{4,0,3,2,1:T(2,128)(2,1)S(1)} copy(bf16[2,1,14,14,1024]{3,0,2,1,4:T(2,128)(2,1)} %bitcast.85) | data formatting | bytes 1605632 | tf_op jit(solution)/shard_map/all_to_all | solution.py:56
  241.7 1.2 pad_bitcast_fusion.1
  242.9 4.0 while.26
  242.9 1.2 dynamic-slice_bitcast_fusion.6
  246.9 31.9 %all-reduce.11 = bf16[2,8,7,7,128]{4,1,0,3,2:T(8,128)(2,1)S(1)} all-reduce(f32[2,8,7,7,128]{4,1,0,3,2:T(8,128)S(1)} %get-tuple-element.61), channel_id=1, replica_groups=mesh['img'=8,'cin'=8,'cout'=8] {'img'}, use_global_device_ids=true, to_apply=%region_3.4 | all-reduce | flops 100352 | bytes 602112 | tf_op jit(solution)/shard_map/psum | solution.py:63
  279.6 41.6 %all-gather.2.cloned.1.call-done = bf16[2,8,7,7,1024]{4,1,0,3,2:T(8,128)(2,1)} async-done(((bf16[2,8,7,7,128]{4,1,0,3,2:T(8,128)(2,1)}), bf16[2,8,7,7,1024]{4,1,0,3,2:T(8,128)(2,1)}) %all-gather.2.cloned.1.call-update) | async-done | bytes 1605648 | tf_op jit(solution)/shard_map/all_gather | solution.py:65
  321.2 3.3 pad_bitcast_fusion
  324.5 17.2 %while.27 = (s32[]{:T(128)}, bf16[2,8,7,7,128]{4,0,3,2,1:T(2,128)(2,1)S(1)}, bf16[2,8,9,9,1024]{4,1,0,3,2:T(8,128)(2,1)}, bf16[9216,128]{1,0:T(8,128)(2,1)S(1)}) while((s32[]{:T(128)}, bf16[2,8,7,7,128]{4,0,3,2,1:T(2,128)(2,1)S(1)}, bf16[2,8,9,9,1024]{4,1,0,3,2:T(8,128)(2,1)}, bf16[9216,128]{1,0:T(8,128)(2,1)S(1)}) %tuple.60), condition=%wide.region_5.6_spmd.clone, body=%wide.region_4.5_spmd.sunk.clone | while | flops 924844032 | bytes 27191356 | solution.py:34
  324.5 1.4 dynamic-slice_bitcast_fusion.7
  326.5 2.0 fusion.29
  328.7 4.4 dynamic_update_slice.16
  333.1 1.4 dynamic-slice_bitcast_fusion.7
  335.1 2.0 fusion.29
  337.3 4.4 dynamic_update_slice.16
  342.5 1.3 dynamic-slice.2
  343.7 109.5 %all-reduce.10.cloned.1.call-done = bf16[2,8,7,7,128]{4,0,3,2,1:T(2,128)(2,1)} async-done(((bf16[2,8,7,7,128]{4,0,3,2,1:T(2,128)(2,1)}), bf16[2,8,7,7,128]{4,0,3,2,1:T(2,128)(2,1)}) %all-reduce.10.cloned.1.call-update) | async-done | bytes 200720
  453.3 1.9 constant_dynamic-slice_fusion
  (73 shorter events, 10.3 us)
Async XLA Ops:
  6.5 1.6 copy-start
  6.5 119.4 %all-reduce.8.cloned.1.call-start = ((), (), s32[]{:S(2)}) async-start(), calls=%async_computation.1 | async-start | bytes 458752 | tf_op jit(solution)/shard_map/psum | solution.py:52
  178.7 24.8 %all-to-all-start = ((bf16[8,2,25088]{2,1,0:T(2,128)(2,1)}), bf16[8,2,25088]{2,1,0:T(2,128)(2,1)S(1)}, u32[]{:S(2)}, u32[]{:S(2)}) async-start(bf16[8,2,25088]{2,1,0:T(2,128)(2,1)} %reshape.68), calls=%async_computation | async-start | bytes 1605632 | tf_op jit(solution)/shard_map/all_to_all | solution.py:56
  182.2 139.0 %all-gather.2.cloned.1.call-start = ((), (), s32[]{:S(2)}) async-start(), calls=%async_computation.2 | async-start | bytes 1806336 | tf_op jit(solution)/shard_map/all_gather | solution.py:65
  223.2 19.7 %copy-start.2 = (bf16[3,3,128,128]{3,2,1,0:T(8,128)(2,1)S(1)}, bf16[3,3,128,128]{3,2,1,0:T(8,128)(2,1)}, u32[]{:S(2)}) copy-start(bf16[3,3,128,128]{3,2,1,0:T(8,128)(2,1)} %param.10) | copy-start | bytes 884740
  242.9 81.6 %copy-start.1 = (bf16[3,3,1024,128]{3,2,1,0:T(8,128)(2,1)S(1)}, bf16[3,3,1024,128]{3,2,1,0:T(8,128)(2,1)}, u32[]{:S(2)}) copy-start(bf16[3,3,1024,128]{3,2,1,0:T(8,128)(2,1)} %param.11) | copy-start | bytes 7077892
  279.5 173.7 %all-reduce.10.cloned.1.call-start = ((), (), s32[]{:S(2)}) async-start(), calls=%async_computation.3 | async-start | bytes 401408
  341.8 0.7 copy-start.3
Sparse Core Ops, SparseCore 0:
  10.3 115.6 all-reduce.7
  279.6 41.5 all-gather.1
  342.6 110.6 all-reduce.9
where the time goes:
time: 463 us; the launch traced here: 462 us
  waiting for transfers between devices  289 us (62%)
  local copies, waits for them, and re-layouts  88.5 us (19%)
  blocking collectives  58.4 us (13%)
  between operations  13.3 us (3%)
  matrix products  6.06 us (1%)
    psum x1, waiting for transfers between devices, local(): summed = lax.psum(first_terms, 'cin')  117 us
    unnamed x4, waiting for transfers between devices  110 us
    all_gather x1, waiting for transfers between devices, local(): gathered = lax.all_gather(narrow, 'cout', axis=4, tiled=True)  41.6 us
    unnamed x19, local copies, waits for them, and re-layouts  36.8 us
    psum x1, blocking collectives, local(): summed_wide = lax.psum(reduced, 'img')  31.9 us
    all_gather x1, blocking collectives, local(): whole = lax.all_gather(segment_maps, 'cout', axis=4, tiled=True)  26.5 us
    all_to_all x1, waiting for transfers between devices, local(): lax.all_to_all(whole, 'img', split_axis=4, concat_axis=1, tiled=True)  21.2 us
    all_to_all x1, local copies, waits for them, and re-layouts, local(): lax.all_to_all(whole, 'img', split_axis=4, concat_axis=1, tiled=True)  17.3 us
  transfers between devices with their start and end apart: 4, of which 4 were waited for; matrix products, arithmetic and copies ran while one was open for 0% of the time, Pallas kernels for 0%

commit v1 on v0

--- a/solution.py
+++ b/solution.py
@@ -1,7 +1,17 @@
+import functools
 import jax
 import jax.numpy as jnp
 from jax import lax
 from jax.sharding import PartitionSpec as P
+from jax.lax import all_gather
+
+
+def edit_the_shelves(m, row_axis):
+    y1 = all_gather(m, axis_name=row_axis).sum(axis=0)
+    return y1
+
+
+post_weights_for = functools.partial(edit_the_shelves, row_axis="img")
 
 
 def conv_block(padded, weight_flat, size, step):
@@ -60,7 +70,7 @@
         batches, images, half, half, w_reduce.shape[3]
     )
     out_width = w_wide.shape[3]
-    summed_wide = lax.psum(reduced, "img")
+    summed_wide = post_weights_for(reduced)
     narrow = jnp.maximum(summed_wide, 0.0).astype(jnp.bfloat16)
     gathered = lax.all_gather(narrow, "cout", axis=4, tiled=True)
     flat_all = gathered.reshape(-1, half, half, gathered.shape[4])

time: 463 us -> 478 us (1.032)
  waiting for transfers between devices: 289 us -> 336 us
  blocking collectives: 58.4 us -> 26.5 us
    all_gather x0 -> x1, waiting for transfers between devices: none -> 43.2 us  [edit_the_shelves(): y1 = all_gather(m, axis_name=row_axis).sum(axis=0)]
    psum x1 -> x0, blocking collectives: 31.9 us -> none  [local(): summed_wide = lax.psum(reduced, 'img')]
    unnamed x19 -> x21, local copies, waits for them, and re-layouts: 36.8 us -> 37.6 us
    unnamed x4 -> x5, waiting for transfers between devices: 110 us -> 110 us
  transfers between devices with their start and end apart: 4 -> 5, of which waited for: 4 -> 5; matrix products, arithmetic and copies ran while one was open for 0% -> 0% of each run, Pallas kernels for 0% -> 0%
where the time goes in v1:
time: 478 us; the launch traced here: 477 us
  waiting for transfers between devices  336 us (70%)
  local copies, waits for them, and re-layouts  86.4 us (18%)
  blocking collectives  26.5 us (6%)
  between operations  13.3 us (3%)
  matrix products  6.06 us (1%)
    psum x1, waiting for transfers between devices, local(): summed = lax.psum(first_terms, 'cin')  117 us
    unnamed x5, waiting for transfers between devices  110 us
    all_gather x1, waiting for transfers between devices, local(): gathered = lax.all_gather(narrow, 'cout', axis=4, tiled=True)  45.4 us
    all_gather x1, waiting for transfers between devices, edit_the_shelves(): y1 = all_gather(m, axis_name=row_axis).sum(axis=0)  43.2 us
    unnamed x21, local copies, waits for them, and re-layouts  37.6 us
    all_gather x1, blocking collectives, local(): whole = lax.all_gather(segment_maps, 'cout', axis=4, tiled=True)  26.5 us
    all_to_all x1, waiting for transfers between devices, local(): lax.all_to_all(whole, 'img', split_axis=4, concat_axis=1, tiled=True)  21.2 us
    all_to_all x1, local copies, waits for them, and re-layouts, local(): lax.all_to_all(whole, 'img', split_axis=4, concat_axis=1, tiled=True)  17.3 us
  transfers between devices with their start and end apart: 5, of which 5 were waited for; matrix products, arithmetic and copies ran while one was open for 0% of the time, Pallas kernels for 0%

profile of v1, /device:TPU:64, one launch (start us, length us, event | category | flops | bytes accessed | tf_op | source)
XLA Modules:
  0.0 476.8 jit_solution(7033032719916706997)
XLA Ops:
  9.4 116.6 %all-reduce.7.cloned.1.call-done = f32[2,1,14,14,128]{4,3,2,0,1:T(8,128)} async-done(((f32[2,1,14,14,128]{4,3,2,0,1:T(8,128)}), f32[2,1,14,14,128]{4,3,2,0,1:T(8,128)}) %all-reduce.7.cloned.1.call-update) | async-done | bytes 200720 | tf_op jit(solution)/shard_map/psum | solution.py:62
  126.9 26.5 %all_gather.9 = bf16[2,1,14,14,1024]{4,3,2,0,1:T(8,128)(2,1)S(1)} all-gather(bf16[2,1,14,14,128]{4,3,2,0,1:T(8,128)(2,1)S(1)} %add_convert_fusion), channel_id=1, replica_groups=mesh['img'=8,'cin'=8,'cout'=8] {'cout'}, dimensions={4}, use_global_device_ids=true | all-gather | bytes 903168 | tf_op jit(solution)/shard_map/all_gather | solution.py:65
  153.5 12.4 %copy.37 = bf16[2,1,14,14,1024]{3,0,2,1,4:T(2,128)(2,1)} copy(bf16[2,1,14,14,1024]{4,3,2,0,1:T(8,128)(2,1)S(1)} %all_gather.9) | data formatting | bytes 1605632 | tf_op jit(solution)/shard_map/all_gather | solution.py:65
  165.9 12.8 %reshape.69 = bf16[8,2,25088]{2,1,0:T(2,128)(2,1)} reshape(bf16[1024,1,14,2,14]{4,3,2,1,0:T(2,128)(2,1)} %bitcast.85) | data formatting | bytes 1605632
  178.7 3.5 all-to-all-start
  182.3 21.2 %all-to-all-done = bf16[8,2,25088]{2,1,0:T(2,128)(2,1)S(1)} async-done(((bf16[8,2,25088]{2,1,0:T(2,128)(2,1)}), bf16[8,2,25088]{2,1,0:T(2,128)(2,1)S(1)}, u32[]{:S(2)}, u32[]{:S(2)}) %all-to-all-start) | async-done | bytes 802848 | tf_op jit(solution)/shard_map/all_to_all | solution.py:66
  203.5 19.8 %reshape.70 = bf16[1024,1,14,2,14]{4,3,2,1,0:T(2,128)(2,1)} reshape(bf16[8,2,25088]{2,1,0:T(2,128)(2,1)S(1)} %all-to-all-done) | data formatting | bytes 1605632
  223.2 17.3 %copy.38 = bf16[2,1,14,14,1024]{4,0,3,2,1:T(2,128)(2,1)S(1)} copy(bf16[2,1,14,14,1024]{3,0,2,1,4:T(2,128)(2,1)} %bitcast.86) | data formatting | bytes 1605632 | tf_op jit(solution)/shard_map/all_to_all | solution.py:66
  242.0 1.9 while.26
  244.7 43.2 %all-gather.6.cloned.1.call-done = f32[16,8,7,7,128]{4,1,3,2,0:T(8,128)} async-done(((f32[2,8,7,7,128]{4,1,3,2,0:T(8,128)}), f32[16,8,7,7,128]{4,1,3,2,0:T(8,128)}) %all-gather.6.cloned.1.call-update) | async-done | bytes 3211280 | tf_op jit(solution)/shard_map/all_gather | solution.py:10
  287.9 2.1 reduce_sum.9
  290.8 45.4 %all-gather.4.cloned.1.call-done = bf16[2,8,7,7,1024]{4,1,3,2,0:T(8,128)(2,1)} async-done(((bf16[2,8,7,7,128]{4,1,3,2,0:T(8,128)(2,1)}), bf16[2,8,7,7,1024]{4,1,3,2,0:T(8,128)(2,1)}) %all-gather.4.cloned.1.call-update) | async-done | bytes 1605648 | tf_op jit(solution)/shard_map/all_gather | solution.py:75
  336.1 1.6 copy.63
  337.7 1.8 pad_bitcast_fusion
  339.5 17.2 %while.27 = (s32[]{:T(128)}, bf16[2,8,7,7,128]{4,0,3,2,1:T(2,128)(2,1)S(1)}, bf16[2,8,9,9,1024]{4,1,0,3,2:T(8,128)(2,1)}, bf16[9216,128]{1,0:T(8,128)(2,1)S(1)}) while((s32[]{:T(128)}, bf16[2,8,7,7,128]{4,0,3,2,1:T(2,128)(2,1)S(1)}, bf16[2,8,9,9,1024]{4,1,0,3,2:T(8,128)(2,1)}, bf16[9216,128]{1,0:T(8,128)(2,1)S(1)}) %tuple.62), condition=%wide.region_5.6_spmd.clone, body=%wide.region_4.5_spmd.sunk.clone | while | flops 924844032 | bytes 27191356 | solution.py:44
  339.5 1.4 dynamic-slice_bitcast_fusion.7
  341.5 2.0 fusion.29
  343.7 4.4 dynamic_update_slice.16
  348.1 1.4 dynamic-slice_bitcast_fusion.7
  350.1 2.0 fusion.29
  352.3 4.4 dynamic_update_slice.16
  357.5 1.3 dynamic-slice.2
  358.7 109.5 %all-reduce.9.cloned.1.call-done = bf16[2,8,7,7,128]{4,0,3,2,1:T(2,128)(2,1)} async-done(((bf16[2,8,7,7,128]{4,0,3,2,1:T(2,128)(2,1)}), bf16[2,8,7,7,128]{4,0,3,2,1:T(2,128)(2,1)}) %all-reduce.9.cloned.1.call-update) | async-done | bytes 200720
  468.2 2.0 constant_dynamic-slice_fusion
  (79 shorter events, 10.4 us)
Async XLA Ops:
  6.5 1.6 copy-start
  6.5 119.4 %all-reduce.7.cloned.1.call-start = ((), (), s32[]{:S(2)}) async-start(), calls=%async_computation.1 | async-start | bytes 458752 | tf_op jit(solution)/shard_map/psum | solution.py:62
  178.7 24.8 %all-to-all-start = ((bf16[8,2,25088]{2,1,0:T(2,128)(2,1)}), bf16[8,2,25088]{2,1,0:T(2,128)(2,1)S(1)}, u32[]{:S(2)}, u32[]{:S(2)}) async-start(bf16[8,2,25088]{2,1,0:T(2,128)(2,1)} %reshape.69), calls=%async_computation | async-start | bytes 1605632 | tf_op jit(solution)/shard_map/all_to_all | solution.py:66
  182.2 105.7 %all-gather.6.cloned.1.call-start = ((), (), s32[]{:S(2)}) async-start(), calls=%async_computation.3 | async-start | bytes 3612672 | tf_op jit(solution)/shard_map/all_gather | solution.py:10
  223.2 18.7 %copy-start.2 = (bf16[3,3,128,128]{3,2,1,0:T(8,128)(2,1)S(1)}, bf16[3,3,128,128]{3,2,1,0:T(8,128)(2,1)}, u32[]{:S(2)}) copy-start(bf16[3,3,128,128]{3,2,1,0:T(8,128)(2,1)} %param.10) | copy-start | bytes 884740
  243.8 0.8 copy-start.3
  243.9 95.7 %copy-start.1 = (bf16[3,3,1024,128]{3,2,1,0:T(8,128)(2,1)S(1)}, bf16[3,3,1024,128]{3,2,1,0:T(8,128)(2,1)}, u32[]{:S(2)}) copy-start(bf16[3,3,1024,128]{3,2,1,0:T(8,128)(2,1)} %param.11) | copy-start | bytes 7077892
  244.6 91.5 %all-gather.4.cloned.1.call-start = ((), (), s32[]{:S(2)}) async-start(), calls=%async_computation.2 | async-start | bytes 1806336 | tf_op jit(solution)/shard_map/all_gather | solution.py:75
  290.7 177.5 %all-reduce.9.cloned.1.call-start = ((), (), s32[]{:S(2)}) async-start(), calls=%async_computation.4 | async-start | bytes 401408
  356.7 0.7 copy-start.4
Sparse Core Ops, SparseCore 0:
  10.3 115.6 all-reduce.6
  244.8 43.0 all-gather.5
  290.8 45.2 all-gather.3
  357.6 110.6 all-reduce.8
